TPU v7x, 32 devices: a whole 2x2x4 slice. The times are simulated.
32 devices in a mesh: groups: 2 (over x), seq: 16 (over z, y, core).
Axes of the slice: x: 2, y: 2, z: 4, core: 2. Of those that a mesh axis runs over, the one named last changes fastest.
Arguments:
- queries: bfloat16 [12288, 2240], P(('groups', 'seq')), parts along dimension 0, may hold values from -6 to 6
- key_rows: bfloat16 [12288, 2240], P(('groups', 'seq')), parts along dimension 0, may hold values from -6 to 6
- value_rows: bfloat16 [12288, 2240], P(('groups', 'seq')), parts along dimension 0, may hold values from -6 to 6
- frame_len: int32 [32, 2], P(('groups', 'seq')), parts along dimension 0, may hold values from 1 to 240, 384 in all within a row
- log_decay: float32 [32, 2, 20], P(('groups', 'seq')), parts along dimension 0, may hold values from -6 to 0
- timestep: int32 [32], P(('groups', 'seq')), parts along dimension 0, may hold values from 0 to 49
- conv_kernel: float32 [4, 2240], replicated, may hold values from -3 to 3
- norm_gain: float32 [2240], replicated, may hold values from 0.1 to 1.9
- mod_table: float32 [50, 2240], replicated, may hold values from -3 to 3
- out_grad: bfloat16 [12288, 2240], P(('groups', 'seq')), parts along dimension 0, may hold values from -6 to 6
Outputs:
- grad_queries: bfloat16 [12288, 2240], P(('groups', 'seq')), parts along dimension 0
- grad_keys: bfloat16 [12288, 2240], P(('groups', 'seq')), parts along dimension 0
- grad_values: bfloat16 [12288, 2240], P(('groups', 'seq')), parts along dimension 0
- grad_kernel: float32 [8, 2240], P('groups'), parts along dimension 0
- grad_gain: float32 [4480], P('groups'), parts along dimension 0
- grad_table: float32 [100, 2240], P('groups'), parts along dimension 0
There are 2 independent parts, one for each index of `groups`. A program takes and returns all parts, laid end to end along the dimension named above; an argument that names none is the same for every part. Nothing has to cross between parts.
Inputs may be any that keep to these rules, and one draw needn't show every extreme that they name: `frame_len`: the 2 frames of each block hold 384 tokens together, and in every block the longest frame has at most 240 tokens.
All inputs are finite; a program needn't handle non-finite values.
Results may differ from a plain program's by a relative error of at most 0.0058.
Values may be sent and summed in bfloat16 or wider, within the bound.
A program may use at most 384 MiB of HBM per device.

v0:
```python
import functools

import jax
import jax.numpy as jnp
from jax import lax
from jax.experimental import pallas as pl
from jax.experimental.pallas import tpu as pltpu
from jax.sharding import PartitionSpec as P

EPSILON = 1e-06
MESH = pl.DeviceIdType.MESH


def scan_kernel(n, rows, head_dim, reverse, *refs):
    if reverse:
        (pieces, extra, decays, out, extra_all, inbox, outbox) = refs[:7]
    else:
        (pieces, extra, out, extra_all, inbox, outbox) = refs[:6]
        decays = extra_all
    (in_send, in_recv, ex_send, ex_recv, out_send, out_recv) = refs[-6:]
    me = lax.axis_index("seq")
    group = lax.axis_index("groups")

    def where(peer):
        return (group, peer)

    def piece_copy(peer, slot):
        return pltpu.make_async_remote_copy(
            src_ref=pieces.at[peer], dst_ref=inbox.at[slot],
            send_sem=in_send.at[peer], recv_sem=in_recv.at[slot],
            device_id=where(peer), device_id_type=MESH)

    def extra_copy(peer, slot):
        return pltpu.make_async_remote_copy(
            src_ref=extra, dst_ref=extra_all.at[slot],
            send_sem=ex_send.at[peer], recv_sem=ex_recv.at[slot],
            device_id=where(peer), device_id_type=MESH)

    def result_copy(peer, slot):
        return pltpu.make_async_remote_copy(
            src_ref=outbox.at[peer], dst_ref=out.at[slot],
            send_sem=out_send.at[peer], recv_sem=out_recv.at[slot],
            device_id=where(peer), device_id_type=MESH)

    barrier = pltpu.get_barrier_semaphore()

    def greet(k, c):
        pl.semaphore_signal(barrier, inc=1, device_id=where(lax.rem(me + k, n)), device_id_type=MESH)
        return c

    lax.fori_loop(1, n, greet, 0)
    inbox[me] = pieces[me]
    extra_all[me] = extra[...]
    pl.semaphore_wait(barrier, n - 1)

    def send(k, c):
        peer = lax.rem(me + k, n)
        extra_copy(peer, me).start()
        piece_copy(peer, me).start()
        return c

    lax.fori_loop(1, n, send, 0)

    lane = lax.broadcasted_iota(jnp.int32, (rows, 128), 1) * head_dim
    index = lax.broadcasted_iota(jnp.int32, (rows, 128), 0) + me * rows
    mine = (index >= lane) & (index < lane + head_dim)

    def step(i, state):
        b = n - 1 - i if reverse else i

        @pl.when(b != me)
        def _():
            extra_copy(b, b).wait_recv()
            piece_copy(b, b).wait_recv()

        outbox[b] = state.astype(jnp.bfloat16)

        @pl.when(b != me)
        def _():
            result_copy(b, me).start()

        row = decays[b]
        factor = jnp.exp(jnp.sum(jnp.where(mine, row, 0.0), axis=1, keepdims=True))
        return factor * state + inbox[b].astype(jnp.float32)

    lax.fori_loop(0, n, step, jnp.zeros(inbox.shape[1:], jnp.float32))
    out[me] = outbox[me]

    def finish(k, c):
        peer = lax.rem(me + k, n)
        extra_copy(peer, peer).wait_send()
        piece_copy(peer, peer).wait_send()
        result_copy(peer, peer).wait_send()
        result_copy(peer, peer).wait_recv()
        return c

    lax.fori_loop(1, n, finish, 0)


def carried(flat, extra, decays, depth, reverse):
    n = lax.axis_size("seq")
    rows, width = flat.shape[0] // n, flat.shape[1]
    pieces = flat.reshape(n, rows, width)
    vmem = pl.BlockSpec(memory_space=pltpu.VMEM)
    args = (pieces, extra) + ((decays,) if reverse else ())
    out, gathered = pl.pallas_call(
        functools.partial(scan_kernel, n, rows, depth, reverse),
        out_shape=(
            jax.ShapeDtypeStruct((n, rows, width), jnp.bfloat16),
            jax.ShapeDtypeStruct((n,) + extra.shape, jnp.float32),
        ),
        in_specs=[vmem] * len(args),
        out_specs=(vmem, vmem),
        scratch_shapes=[pltpu.VMEM((n, rows, width), jnp.bfloat16)] * 2
        + [pltpu.SemaphoreType.DMA((n,))] * 6,
        compiler_params=pltpu.CompilerParams(
            collective_id=1 if reverse else 0, has_side_effects=True, vmem_limit_bytes=48 << 20),
        name="adjoint_scan" if reverse else "state_scan",
    )(*args)
    return out.reshape(n * rows, width), gathered


def tail_kernel(n, terms, edge, total, following, held, landed, send_sem, recv_sem, edge_send, edge_recv):
    me = lax.axis_index("seq")
    group = lax.axis_index("groups")
    steps = n.bit_length() - 1
    barrier = pltpu.get_barrier_semaphore()
    partners = [me + (1 << i) - (2 << i) * ((me // (1 << i)) % 2) for i in range(steps)]
    for partner in partners:
        pl.semaphore_signal(barrier, inc=1, device_id=(group, partner), device_id_type=MESH)
    before, after = lax.rem(me + n - 1, n), lax.rem(me + 1, n)
    for peer in (before, after):
        pl.semaphore_signal(barrier, inc=1, device_id=(group, peer), device_id_type=MESH)
    pl.semaphore_wait(barrier, steps + 2)
    edge_copy = pltpu.make_async_remote_copy(
        src_ref=edge, dst_ref=following, send_sem=edge_send, recv_sem=edge_recv,
        device_id=(group, before), device_id_type=MESH)
    edge_copy.start()
    held[0] = terms[...]
    for i, partner in enumerate(partners):
        copy = pltpu.make_async_remote_copy(
            src_ref=held.at[i], dst_ref=landed.at[i], send_sem=send_sem.at[i], recv_sem=recv_sem.at[i],
            device_id=(group, partner), device_id_type=MESH)
        copy.start()
        copy.wait()
        held[i + 1] = held[i] + landed[i]
    total[...] = held[steps]
    edge_copy.wait()


def tail_exchange(terms, edge):
    n = lax.axis_size("seq")
    steps = n.bit_length() - 1
    vmem = pl.BlockSpec(memory_space=pltpu.VMEM)
    return pl.pallas_call(
        functools.partial(tail_kernel, n),
        out_shape=(jax.ShapeDtypeStruct(terms.shape, jnp.float32), jax.ShapeDtypeStruct(edge.shape, jnp.float32)),
        in_specs=[vmem, vmem],
        out_specs=(vmem, vmem),
        scratch_shapes=[
            pltpu.VMEM((steps + 1,) + terms.shape, jnp.float32),
            pltpu.VMEM((steps,) + terms.shape, jnp.float32),
            pltpu.SemaphoreType.DMA((steps,)),
            pltpu.SemaphoreType.DMA((steps,)),
            pltpu.SemaphoreType.DMA,
            pltpu.SemaphoreType.DMA,
        ],
        compiler_params=pltpu.CompilerParams(collective_id=2, has_side_effects=True),
        name="tail_exchange",
    )(terms, edge)


def passed_along(value, axis):
    count = lax.axis_size(axis)
    return lax.ppermute(value, axis, [(s, s + 1) for s in range(count - 1)])


def mm(a, b, ca, cb):
    return lax.dot_general(a, b, (((ca,), (cb,)), ((), ())), preferred_element_type=jnp.float32)


def framed_outer(left, right, late, w0, w1):
    second = right * late
    first = right - second
    return (w0 * mm(left, first, 1, 1) + w1 * mm(left, second, 1, 1)).astype(jnp.bfloat16)


def per_head(heads, dim, work):
    def pair(i, carry):
        for j in range(2):
            h = i * 2 + j
            work(h, pl.ds(pl.multiple_of(h * dim, 16), dim))
        return carry

    lax.fori_loop(0, heads // 2, pair, 0)
    if heads % 2:
        work(heads - 1, pl.ds((heads - 1) * dim, dim))


def delayed(value, before, taps):
    count = value.shape[1]
    joined = jnp.concatenate([before, value], axis=1)
    width = joined.shape[1]
    return [value] + [pltpu.roll(joined, j, 1)[:, width - count :] for j in range(1, taps)]


def pre_kernel(heads, dim, tap_count, scal, late, key, value, before, columns, conv, state):
    def work(h, c):
        x = delayed(value[c, :].astype(jnp.float32), before[c, :].astype(jnp.float32), tap_count)
        cols = columns[c, :]
        total = cols[:, 0:1] * x[0]
        for j in range(1, tap_count):
            total = total + cols[:, j : j + 1] * x[j]
        v = total.astype(jnp.bfloat16)
        conv[c, :] = v
        state[c, :] = framed_outer(v, key[c, :], late[...], scal[0, h], 1.0)

    per_head(heads, dim, work)
    state[heads * dim :, :] = jnp.zeros_like(state[heads * dim :, :])


def mid_kernel(heads, dim, tap_count, scal, late, same, cross, query, key, conv, upstream, columns, state,
               grad_query, key_part, value_part, adjoint, terms):
    is_late = late[0:1, :].astype(jnp.float32) > 0.5

    def work(h, c):
        q, k, v, s_in = query[c, :], key[c, :], conv[c, :], state[c, :]
        row_scale = jnp.where(is_late, scal[2, h], scal[1, h])
        weight = same[...] + scal[0, h] * cross[...]
        attn = (mm(k, q, 0, 0) * weight).astype(jnp.bfloat16)
        numerator = mm(v, attn, 1, 0) + row_scale * mm(s_in, q, 1, 0)
        inv_rms = lax.rsqrt(jnp.mean(numerator * numerator, axis=0, keepdims=True) + EPSILON)
        normed = numerator * inv_rms
        up = upstream[c, :].astype(jnp.float32)
        terms[c, :] = jnp.sum(up * normed, axis=1, keepdims=True)
        normed_grad = up * columns[c, :][:, tap_count : tap_count + 1]
        g = (inv_rms * (
            normed_grad - normed * jnp.mean(normed_grad * normed, axis=0, keepdims=True)
        )).astype(jnp.bfloat16)
        adjoint[c, :] = framed_outer(g, q, late[...], scal[1, h], scal[2, h])
        score = (mm(v, g, 0, 0) * weight).astype(jnp.bfloat16)
        grad_query[c, :] = (mm(k, score, 1, 0) + row_scale * mm(s_in, g, 0, 0)).astype(jnp.bfloat16)
        key_part[c, :] = mm(q, score, 1, 1)
        value_part[c, :] = mm(g, attn, 1, 1)

    per_head(heads, dim, work)
    adjoint[heads * dim :, :] = jnp.zeros_like(adjoint[heads * dim :, :])


def post_kernel(heads, dim, tap_count, scal, late, key, conv, value, before, columns, adjoint, key_part,
                value_part, grad_key, grad_value, tap_terms, opening, ending):
    is_late = late[0:1, :].astype(jnp.float32) > 0.5

    def work(h, c):
        into_end = jnp.where(is_late, 1.0, scal[0, h])
        adj = adjoint[c, :]
        grad_key[c, :] = (key_part[c, :] + into_end * mm(adj, conv[c, :], 0, 0)).astype(jnp.bfloat16)
        own = value_part[c, :] + into_end * mm(adj, key[c, :], 1, 0)
        opening[c, :] = own[:, :128]
        count = own.shape[1]
        x = delayed(value[c, :].astype(jnp.float32), before[c, :].astype(jnp.float32), tap_count)
        joined = jnp.concatenate([own, jnp.zeros((dim, 128), jnp.float32)], axis=1)
        cols = columns[c, :]
        total = cols[:, 0:1] * own
        tap_terms[c, 0:1] = jnp.sum(own * x[0], axis=1, keepdims=True)
        for j in range(1, tap_count):
            total = total + cols[:, j : j + 1] * pltpu.roll(joined, count + 128 - j, 1)[:, :count]
            tap_terms[c, j : j + 1] = jnp.sum(own * x[j], axis=1, keepdims=True)
        grad_value[c, :] = total.astype(jnp.bfloat16)
        ending[c, :] = total[:, count - 128 :]

    per_head(heads, dim, work)


def local_call(kernel, name, args, outs, scratch=()):
    vmem = pl.BlockSpec(memory_space=pltpu.VMEM)
    return pl.pallas_call(
        kernel,
        out_shape=tuple(outs),
        in_specs=[pl.BlockSpec(memory_space=pltpu.SMEM)] + [vmem] * (len(args) - 1),
        out_specs=tuple([vmem] * len(outs)),
        scratch_shapes=list(scratch),
        compiler_params=pltpu.CompilerParams(vmem_limit_bytes=56 << 20),
        name=name,
    )(*args)


def body(
    queries,
    key_rows,
    value_rows,
    frame_len,
    log_decay,
    timestep,
    conv_kernel,
    norm_gain,
    mod_table,
    out_grad,
):
    f32, bf16 = jnp.float32, jnp.bfloat16
    shape = jax.ShapeDtypeStruct
    row_count, channels = queries.shape
    head_count = log_decay.shape[2]
    head_dim = channels // head_count
    score_scale = head_dim ** (-0.5)
    tap_count = conv_kernel.shape[0]
    block_count = lax.axis_size("seq")
    place = lax.axis_index("seq")
    state_rows = -(-channels // (16 * block_count)) * 16 * block_count

    span = tap_count - 1
    previous = passed_along(value_rows[row_count - span :], "seq")
    before = jnp.pad(previous.T, ((0, 0), (128 - span, 0)))
    query_t, key_t, value_t, upstream_t = (a.T for a in (queries, key_rows, value_rows, out_grad))
    cum0 = log_decay[0, 0]
    cum1 = cum0 + log_decay[0, 1]
    scal = jnp.stack([jnp.exp(cum1 - cum0), score_scale * jnp.exp(cum0), score_scale * jnp.exp(cum1)])
    first = frame_len[0, 0]
    late_at = lambda size, axis: lax.broadcasted_iota(jnp.int32, size, axis) >= first
    late = late_at((head_dim, row_count), 1).astype(bf16)
    square = (row_count, row_count)
    late_s, late_t = late_at(square, 0), late_at(square, 1)
    same = jnp.where(late_t == late_s, score_scale, 0.0).astype(f32)
    cross = jnp.where(late_t & ~late_s, score_scale, 0.0).astype(f32)
    levels = jnp.arange(mod_table.shape[0], dtype=jnp.int32)
    mod_row = lax.dynamic_index_in_dim(mod_table, timestep[0], 0, True)
    gain = norm_gain[None, :] * (1.0 + mod_row)
    columns = jnp.concatenate([conv_kernel, gain], axis=0).T
    lanes = jnp.concatenate([
        cum1, timestep.astype(f32), jnp.zeros((128 - head_count - 1,), f32)])[None, :]

    sizes = (head_count, head_dim, tap_count)
    whole = (channels, row_count)
    conv_values, local_state = local_call(
        functools.partial(pre_kernel, *sizes), "conv_state",
        (scal, late, key_t, value_t, before, columns),
        (shape(whole, bf16), shape((state_rows, head_dim), bf16)))
    state_in, gathered = carried(local_state, lanes, None, head_dim, False)
    query_grad, key_part, value_part, adjoint_local, block_terms = local_call(
        functools.partial(mid_kernel, *sizes), "heads",
        (scal, late, same, cross, query_t, key_t, conv_values, upstream_t, columns, state_in),
        (shape(whole, bf16), shape(whole, f32), shape(whole, f32),
         shape((state_rows, head_dim), bf16), shape((channels, 1), f32)))
    adjoint, terms_all = carried(adjoint_local, block_terms.reshape(1, channels), gathered, head_dim, True)
    key_grad, value_grad, tap_terms, opening, ending = local_call(
        functools.partial(post_kernel, *sizes), "adjoint_terms",
        (scal, late, key_t, conv_values, value_t, before, columns, adjoint, key_part, value_part),
        (shape(whole, bf16), shape(whole, bf16), shape((channels, tap_count), f32),
         shape((channels, 128), f32), shape((channels, 128), f32)))
    kernel_sum, following = tail_exchange(tap_terms.T, opening[:, :span].T)
    following = jnp.where(place == block_count - 1, 0.0, following).T
    fixed = []
    for i in range(span):
        column = ending[:, 128 - span + i]
        for j in range(span - i, tap_count):
            column = column + conv_kernel[j] * following[:, i + j - span]
        fixed.append(column)
    value_grad = lax.dynamic_update_slice(
        value_grad, jnp.stack(fixed, axis=1).astype(bf16), (0, row_count - span))
    query_grad, key_grad, value_grad = query_grad.T, key_grad.T, value_grad.T
    terms = terms_all[:, 0, :]
    chosen = (gathered[:, 0, head_count].astype(jnp.int32)[:, None] == levels[None, :]).astype(f32)
    sums = jnp.einsum("bl,bc->lc", chosen, terms, precision=lax.Precision.HIGHEST)
    gain_sum = jnp.sum(sums * (1.0 + mod_table), axis=0)
    table_sum = sums * norm_gain
    return (
        query_grad,
        key_grad,
        value_grad,
        kernel_sum / block_count,
        gain_sum / block_count,
        table_sum / block_count,
    )


def solution(mesh):
    in_specs = (
        P(("groups", "seq"), None),
        P(("groups", "seq"), None),
        P(("groups", "seq"), None),
        P(("groups", "seq"), None),
        P(("groups", "seq"), None, None),
        P(("groups", "seq")),
        P(),
        P(),
        P(),
        P(("groups", "seq"), None),
    )
    out_specs = (
        P(("groups", "seq"), None),
        P(("groups", "seq"), None),
        P(("groups", "seq"), None),
        P("groups", None),
        P("groups"),
        P("groups", None),
    )
    return jax.shard_map(body, mesh=mesh, in_specs=in_specs, out_specs=out_specs, check_vma=False)
```

profile of v0, /device:TPU:0, one launch (start us, length us, event | category | flops | bytes accessed | tf_op | source)
XLA Modules:
  0.0 177.4 jit_solution(14401553789363330855)
XLA Ops:
  0.7 1.3 slice.54
  2.0 0.3 copy.43
  2.3 2.4 %collective-permute-start = (bf16[3,2240]{1,0:T(4,128)(2,1)S(1)}, bf16[3,2240]{1,0:T(4,128)(2,1)S(1)}, u32[]{:S(2)}, u32[]{:S(2)}) collective-permute-start(bf16[3,2240]{1,0:T(4,128)(2,1)S(1)} %copy.43), channel_id=1, source_target_pairs={{0,1},{1,2},{2,3},{3,4},{4,5},{5,6},{6,7},{7,8},{8,9},{9,10},{10,1... | collective-permute-start | bytes 40328 | tf_op jit(solution)/shard_map/ppermute | solution.py:175
  5.5 1.2 and_select_fusion
  6.7 0.6 pad_maximum_fusion.2.scal
  7.3 1.5 copy.35
  8.8 0.4 copy.34
  9.2 1.1 pad.4.before
  10.3 0.6 iota.21.late
  10.9 9.9 %conv_state.1 = (bf16[2240,384]{1,0:T(8,128)(2,1)}, bf16[2304,112]{1,0:T(8,128)(2,1)}) custom-call(f32[3,20]{1,0:T(4,128)} %pad_maximum_fusion.2.scal, bf16[112,384]{1,0:T(8,128)(2,1)} %iota.21.late, bf16[2240,384]{1,0:T(8,128)(2,1)} %bitcast.87, bf16[2240,384]{1,0:T(8,128)(2,1)} %bitcast.90, bf16[2240,128]{1,0:T(8,128)(2,1)} %pad.4.before, f32[2240,5]{1,0:T(8,128)} %bitcast.84), custom_call_target="tpu_custom_call" | custom-call | tf_op jit(solution)/shard_map/conv_state/pallas_call | solution.py:277
  20.8 1.1 copy-done.3
  21.9 28.8 %state_scan.1 = (bf16[16,144,112]{2,1,0:T(8,128)(2,1)S(1)}, f32[16,1,128]{2,1,0:T(1,128)S(1)}) custom-call(bf16[16,144,112]{2,1,0:T(8,128)(2,1)S(1)} %bitcast.83, f32[1,128]{1,0:T(1,128)S(1)} %maximum_bitcast_fusion.refs_1_), custom_call_target="tpu_custom_call" | custom-call | tf_op jit(solution)/shard_map/state_scan/pallas_call | solution.py:106
  50.7 0.8 copy-done.1
  51.5 0.4 convert_reduce_fusion
  52.0 28.6 %heads.1 = (bf16[2240,384]{1,0:T(8,128)(2,1)}, f32[2240,384]{1,0:T(8,128)}, f32[2240,384]{1,0:T(8,128)}, bf16[2304,112]{1,0:T(8,128)(2,1)}, f32[2240,1]{1,0:T(8,128)}) custom-call(f32[3,20]{1,0:T(4,128)} %pad_maximum_fusion.2.scal, bf16[112,384]{1,0:T(8,128)(2,1)} %iota.21.late, f32[384,384]{1,0:T(8,128)} %get-tuple-element.51.same, ...), custom_call_target="tpu_custom_call" | custom-call | tf_op jit(solution)/shard_map/heads/pallas_call | solution.py:277
  80.6 1.6 reduce
  82.2 1.1 copy-done.2
  83.3 42.7 %adjoint_scan.1 = (bf16[16,144,112]{2,1,0:T(8,128)(2,1)S(1)}, f32[16,1,2240]{2,1,0:T(1,128)S(1)}) custom-call(bf16[16,144,112]{2,1,0:T(8,128)(2,1)S(1)} %bitcast.82, f32[1,2240]{1,0:T(1,128)S(1)} %reshape.100.refs_1_, f32[16,1,128]{2,1,0:T(1,128)S(1)} %get-tuple-element.30.refs_2_), custom_call_target="tpu_custom_call" | custom-call | tf_op jit(solution)/shard_map/adjoint_scan/pallas_call | solution.py:106
  125.9 0.8 copy-done
  126.8 21.2 %adjoint_terms.1 = (bf16[2240,384]{1,0:T(8,128)(2,1)}, bf16[2240,384]{1,0:T(8,128)(2,1)}, f32[2240,4]{1,0:T(8,128)}, f32[2240,128]{1,0:T(8,128)}, f32[2240,128]{1,0:T(8,128)}) custom-call(f32[3,20]{1,0:T(4,128)} %pad_maximum_fusion.2.scal, bf16[112,384]{1,0:T(8,128)(2,1)} %iota.21.late, bf16[2240,384]{1,0:T(8,128)(2,1)} %bitcast.89, ...), custom_call_target="tpu_custom_call" | custom-call | tf_op jit(solution)/shard_map/adjoint_terms/pallas_call | solution.py:277
  147.9 2.3 %copy.37 = f32[2240,4]{0,1:T(4,128)} copy(f32[2240,4]{1,0:T(8,128)} %get-tuple-element.37) | data formatting | bytes 71680 | tf_op jit(solution)/shard_map/adjoint_terms/pallas_call | solution.py:277
  150.3 1.4 multiply_multiply_fusion
  151.6 0.6 broadcast_multiply_fusion.1
  152.2 0.4 copy.36
  152.6 0.4 copy.38
  153.0 0.6 slice_bitcast_fusion.edge
  153.6 14.1 %tail_exchange.1 = (f32[4,2240]{1,0:T(4,128)}, f32[3,2240]{1,0:T(4,128)}) custom-call(f32[4,2240]{1,0:T(4,128)} %bitcast.95, f32[3,2240]{1,0:T(4,128)} %slice_bitcast_fusion.edge), custom_call_target="tpu_custom_call" | custom-call | tf_op jit(solution)/shard_map/tail_exchange/pallas_call | solution.py:155
  167.8 1.4 broadcast_multiply_fusion
  169.1 0.8 select_bitcast_fusion
  169.9 0.1 fusion.6
  170.1 0.3 copy.41
  170.4 7.0 %dynamic_update_slice.3 = bf16[2240,384]{1,0:T(8,128)(2,1)} dynamic-update-slice(bf16[2240,384]{1,0:T(8,128)(2,1)} %get-tuple-element.35, bf16[2240,3]{1,0:T(8,128)(2,1)S(1)} %copy.41, s32[]{:T(128)} %constant.13.clone.1, s32[]{:T(128)} %constant.9.clone.1) | dynamic-update-slice | bytes 26884 | tf_op jit(solution)/shard_map/dynamic_update_slice | solution.py:358
  (29 shorter events, 0.3 us)
Async XLA Ops:
  0.6 4.0 %copy-start.10 = (s32[1,2]{1,0:T(1,128)S(1)}, s32[1,2]{1,0:T(1,128)}, u32[]{:S(2)}) copy-start(s32[1,2]{1,0:T(1,128)} %param.13) | copy-start | bytes 28
  0.6 4.1 %copy-start.9 = (f32[1,2,20]{2,1,0:T(2,128)S(1)}, f32[1,2,20]{2,1,0:T(2,128)}, u32[]{:S(2)}) copy-start(f32[1,2,20]{2,1,0:T(2,128)} %param.14) | copy-start | bytes 484
  0.7 4.8 %copy-start.6 = (f32[50,2240]{1,0:T(8,128)S(1)}, f32[50,2240]{1,0:T(8,128)}, u32[]{:S(2)}) copy-start(f32[50,2240]{1,0:T(8,128)} %param.18) | copy-start | bytes 1344004
  0.7 4.8 %copy-start.8 = (f32[2240]{0:T(1024)S(1)}, f32[2240]{0:T(1024)}, u32[]{:S(2)}) copy-start(f32[2240]{0:T(1024)} %param.17) | copy-start | bytes 26884
  0.7 4.8 %copy-start.7 = (f32[4,2240]{1,0:T(4,128)S(1)}, f32[4,2240]{1,0:T(4,128)}, u32[]{:S(2)}) copy-start(f32[4,2240]{1,0:T(4,128)} %param.16) | copy-start | bytes 107524
  2.3 6.6 %collective-permute-start = (bf16[3,2240]{1,0:T(4,128)(2,1)S(1)}, bf16[3,2240]{1,0:T(4,128)(2,1)S(1)}, u32[]{:S(2)}, u32[]{:S(2)}) collective-permute-start(bf16[3,2240]{1,0:T(4,128)(2,1)S(1)} %copy.43), channel_id=1, source_target_pairs={{0,1},{1,2},{2,3},{3,4},{4,5},{5,6},{6,7},{7,8},{8,9},{9,10},{10,1... | collective-permute-start | bytes 40328 | tf_op jit(solution)/shard_map/ppermute | solution.py:175
  20.8 1.1 copy-start.3
  50.7 0.8 copy-start.1
  82.2 1.1 copy-start.2
  125.9 0.8 copy-start
  147.9 4.3 %copy-start.5 = (f32[2240,128]{1,0:T(8,128)S(1)}, f32[2240,128]{1,0:T(8,128)}, u32[]{:S(2)}) copy-start(f32[2240,128]{1,0:T(8,128)} %get-tuple-element.36) | copy-start | bytes 3440644
  150.3 2.3 %copy-start.4 = (f32[2240,128]{1,0:T(8,128)S(1)}, f32[2240,128]{1,0:T(8,128)}, u32[]{:S(2)}) copy-start(f32[2240,128]{1,0:T(8,128)} %get-tuple-element.38) | copy-start | bytes 3440644
where the time goes:
time: 178 us; the launch traced here: 177 us
  Pallas kernels  145 us (81%)
  local copies, waits for them, and re-layouts  19.9 us (11%)
  other arithmetic  6.92 us (4%)
  starting transfers between devices  2.36 us (1%)
    pallas_call x2, Pallas kernels, carried(): pl.pallas_call(functools.partial(scan_kernel, n, rows, depth, reverse), o...  71.5 us
    pallas_call x3, Pallas kernels, local_call(): pl.pallas_call(kernel, out_shape=tuple(outs), in_specs=[pl.BlockSpec(memo...  59.7 us
    pallas_call x1, Pallas kernels, tail_exchange(): pl.pallas_call(functools.partial(tail_kernel, n), out_shape=(jax.ShapeDty...  14.1 us
    dynamic_update_slice x1, local copies, waits for them, and re-layouts, body(): lax.dynamic_update_slice(value_grad, jnp.stack(fixed, axis=1).astype(bf16...  6.97 us
    unnamed x23, local copies, waits for them, and re-layouts  4.05 us
  transfers between devices with their start and end apart: 1, of which 0 were waited for; matrix products, arithmetic and copies ran while one was open for 2% of the time, Pallas kernels for 0%

commit v1 on v0

--- a/solution.py
+++ b/solution.py
@@ -11,7 +11,10 @@
 MESH = pl.DeviceIdType.MESH
 
 
-def scan_kernel(n, rows, head_dim, reverse, *refs):
+def scan_kernel(n, rows, heads, head_dim, reverse, work, ins, outs, *refs):
+    lead = 3 if reverse else 2
+    work = functools.partial(work, *refs[lead : lead + ins], *refs[lead + ins + 2 : lead + ins + 2 + outs])
+    refs = refs[:lead] + refs[lead + ins : lead + ins + 2] + refs[lead + ins + 2 + outs :]
     if reverse:
         (pieces, extra, decays, out, extra_all, inbox, outbox) = refs[:7]
     else:
@@ -61,6 +64,8 @@
 
     lax.fori_loop(1, n, send, 0)
 
+    half = heads // 4 * 2
+    per_head(0, half, head_dim, work)
     lane = lax.broadcasted_iota(jnp.int32, (rows, 128), 1) * head_dim
     index = lax.broadcasted_iota(jnp.int32, (rows, 128), 0) + me * rows
     mine = (index >= lane) & (index < lane + head_dim)
@@ -85,6 +90,7 @@
 
     lax.fori_loop(0, n, step, jnp.zeros(inbox.shape[1:], jnp.float32))
     out[me] = outbox[me]
+    per_head(half, heads, head_dim, work)
 
     def finish(k, c):
         peer = lax.rem(me + k, n)
@@ -97,27 +103,28 @@
     lax.fori_loop(1, n, finish, 0)
 
 
-def carried(flat, extra, decays, depth, reverse):
+def carried(flat, extra, decays, heads, depth, reverse, work, work_args, work_outs):
     n = lax.axis_size("seq")
     rows, width = flat.shape[0] // n, flat.shape[1]
     pieces = flat.reshape(n, rows, width)
     vmem = pl.BlockSpec(memory_space=pltpu.VMEM)
-    args = (pieces, extra) + ((decays,) if reverse else ())
-    out, gathered = pl.pallas_call(
-        functools.partial(scan_kernel, n, rows, depth, reverse),
+    args = (pieces, extra) + ((decays,) if reverse else ()) + tuple(work_args)
+    out, gathered, *results = pl.pallas_call(
+        functools.partial(scan_kernel, n, rows, heads, depth, reverse, work, len(work_args), len(work_outs)),
         out_shape=(
             jax.ShapeDtypeStruct((n, rows, width), jnp.bfloat16),
             jax.ShapeDtypeStruct((n,) + extra.shape, jnp.float32),
-        ),
-        in_specs=[vmem] * len(args),
-        out_specs=(vmem, vmem),
+        ) + tuple(work_outs),
+        in_specs=[vmem] * (len(args) - len(work_args)) + [pl.BlockSpec(memory_space=pltpu.SMEM)]
+        + [vmem] * (len(work_args) - 1),
+        out_specs=(vmem,) * (2 + len(work_outs)),
         scratch_shapes=[pltpu.VMEM((n, rows, width), jnp.bfloat16)] * 2
         + [pltpu.SemaphoreType.DMA((n,))] * 6,
         compiler_params=pltpu.CompilerParams(
             collective_id=1 if reverse else 0, has_side_effects=True, vmem_limit_bytes=48 << 20),
         name="adjoint_scan" if reverse else "state_scan",
     )(*args)
-    return out.reshape(n * rows, width), gathered
+    return (out.reshape(n * rows, width), gathered, *results)
 
 
 def tail_kernel(n, terms, edge, total, following, held, landed, send_sem, recv_sem, edge_send, edge_recv):
@@ -185,16 +192,16 @@
     return (w0 * mm(left, first, 1, 1) + w1 * mm(left, second, 1, 1)).astype(jnp.bfloat16)
 
 
-def per_head(heads, dim, work):
+def per_head(start, stop, dim, work):
     def pair(i, carry):
         for j in range(2):
             h = i * 2 + j
             work(h, pl.ds(pl.multiple_of(h * dim, 16), dim))
         return carry
 
-    lax.fori_loop(0, heads // 2, pair, 0)
-    if heads % 2:
-        work(heads - 1, pl.ds((heads - 1) * dim, dim))
+    lax.fori_loop(start // 2, stop // 2, pair, 0)
+    if stop % 2:
+        work(stop - 1, pl.ds((stop - 1) * dim, dim))
 
 
 def delayed(value, before, taps):
@@ -215,20 +222,34 @@
         conv[c, :] = v
         state[c, :] = framed_outer(v, key[c, :], late[...], scal[0, h], 1.0)
 
-    per_head(heads, dim, work)
+    per_head(0, heads, dim, work)
     state[heads * dim :, :] = jnp.zeros_like(state[heads * dim :, :])
 
 
-def mid_kernel(heads, dim, tap_count, scal, late, same, cross, query, key, conv, upstream, columns, state,
-               grad_query, key_part, value_part, adjoint, terms):
+def ahead_work(scal, same, cross, query, key, conv, part, h, c):
+    weight = same[...] + scal[0, h] * cross[...]
+    attn = (mm(key[c, :], query[c, :], 0, 0) * weight).astype(jnp.bfloat16)
+    part[c, :] = mm(conv[c, :], attn, 1, 0)
+
+
+def back_work(scal, late, same, cross, query, key, conv, grad, state, grad_query, key_part, value_part, h, c):
+    row_scale = jnp.where(late[0:1, :].astype(jnp.float32) > 0.5, scal[2, h], scal[1, h])
+    q, k, g = query[c, :], key[c, :], grad[c, :]
+    weight = same[...] + scal[0, h] * cross[...]
+    attn = (mm(k, q, 0, 0) * weight).astype(jnp.bfloat16)
+    score = (mm(conv[c, :], g, 0, 0) * weight).astype(jnp.bfloat16)
+    grad_query[c, :] = (mm(k, score, 1, 0) + row_scale * mm(state[c, :], g, 0, 0)).astype(jnp.bfloat16)
+    key_part[c, :] = mm(q, score, 1, 1)
+    value_part[c, :] = mm(g, attn, 1, 1)
+
+
+def mid_kernel(heads, dim, tap_count, scal, late, query, part, upstream, columns, state, grad, adjoint, terms):
     is_late = late[0:1, :].astype(jnp.float32) > 0.5
 
     def work(h, c):
-        q, k, v, s_in = query[c, :], key[c, :], conv[c, :], state[c, :]
+        q = query[c, :]
         row_scale = jnp.where(is_late, scal[2, h], scal[1, h])
-        weight = same[...] + scal[0, h] * cross[...]
-        attn = (mm(k, q, 0, 0) * weight).astype(jnp.bfloat16)
-        numerator = mm(v, attn, 1, 0) + row_scale * mm(s_in, q, 1, 0)
+        numerator = part[c, :] + row_scale * mm(state[c, :], q, 1, 0)
         inv_rms = lax.rsqrt(jnp.mean(numerator * numerator, axis=0, keepdims=True) + EPSILON)
         normed = numerator * inv_rms
         up = upstream[c, :].astype(jnp.float32)
@@ -237,13 +258,10 @@
         g = (inv_rms * (
             normed_grad - normed * jnp.mean(normed_grad * normed, axis=0, keepdims=True)
         )).astype(jnp.bfloat16)
+        grad[c, :] = g
         adjoint[c, :] = framed_outer(g, q, late[...], scal[1, h], scal[2, h])
-        score = (mm(v, g, 0, 0) * weight).astype(jnp.bfloat16)
-        grad_query[c, :] = (mm(k, score, 1, 0) + row_scale * mm(s_in, g, 0, 0)).astype(jnp.bfloat16)
-        key_part[c, :] = mm(q, score, 1, 1)
-        value_part[c, :] = mm(g, attn, 1, 1)
-
-    per_head(heads, dim, work)
+
+    per_head(0, heads, dim, work)
     adjoint[heads * dim :, :] = jnp.zeros_like(adjoint[heads * dim :, :])
 
 
@@ -269,7 +287,11 @@
         grad_value[c, :] = total.astype(jnp.bfloat16)
         ending[c, :] = total[:, count - 128 :]
 
-    per_head(heads, dim, work)
+    per_head(0, heads, dim, work)
+
+
+def end_kernel(whole, tile, out):
+    out[...] = tile[...].astype(jnp.bfloat16)
 
 
 def local_call(kernel, name, args, outs, scratch=()):
@@ -335,13 +357,17 @@
         functools.partial(pre_kernel, *sizes), "conv_state",
         (scal, late, key_t, value_t, before, columns),
         (shape(whole, bf16), shape((state_rows, head_dim), bf16)))
-    state_in, gathered = carried(local_state, lanes, None, head_dim, False)
-    query_grad, key_part, value_part, adjoint_local, block_terms = local_call(
+    state_in, gathered, part = carried(
+        local_state, lanes, None, head_count, head_dim, False, ahead_work,
+        (scal, same, cross, query_t, key_t, conv_values), (shape(whole, f32),))
+    grad, adjoint_local, block_terms = local_call(
         functools.partial(mid_kernel, *sizes), "heads",
-        (scal, late, same, cross, query_t, key_t, conv_values, upstream_t, columns, state_in),
-        (shape(whole, bf16), shape(whole, f32), shape(whole, f32),
-         shape((state_rows, head_dim), bf16), shape((channels, 1), f32)))
-    adjoint, terms_all = carried(adjoint_local, block_terms.reshape(1, channels), gathered, head_dim, True)
+        (scal, late, query_t, part, upstream_t, columns, state_in),
+        (shape(whole, bf16), shape((state_rows, head_dim), bf16), shape((channels, 1), f32)))
+    adjoint, terms_all, query_grad, key_part, value_part = carried(
+        adjoint_local, block_terms.reshape(1, channels), gathered, head_count, head_dim, True, back_work,
+        (scal, late, same, cross, query_t, key_t, conv_values, grad, state_in),
+        (shape(whole, bf16), shape(whole, f32), shape(whole, f32)))
     key_grad, value_grad, tap_terms, opening, ending = local_call(
         functools.partial(post_kernel, *sizes), "adjoint_terms",
         (scal, late, key_t, conv_values, value_t, before, columns, adjoint, key_part, value_part),
@@ -351,12 +377,20 @@
     following = jnp.where(place == block_count - 1, 0.0, following).T
     fixed = []
     for i in range(span):
-        column = ending[:, 128 - span + i]
+        column = jnp.zeros((channels,), f32)
         for j in range(span - i, tap_count):
             column = column + conv_kernel[j] * following[:, i + j - span]
         fixed.append(column)
-    value_grad = lax.dynamic_update_slice(
-        value_grad, jnp.stack(fixed, axis=1).astype(bf16), (0, row_count - span))
+    tile = ending + jnp.pad(jnp.stack(fixed, axis=1), ((0, 0), (128 - span, 0)))
+    value_grad = pl.pallas_call(
+        end_kernel,
+        grid=(1,),
+        out_shape=shape(whole, bf16),
+        in_specs=[pl.BlockSpec(memory_space=pl.ANY), pl.BlockSpec((channels, 128), lambda i: (0, 0))],
+        out_specs=pl.BlockSpec((channels, 128), lambda i: (0, row_count // 128 - 1)),
+        input_output_aliases={0: 0},
+        name="last_tokens",
+    )(value_grad, tile)
     query_grad, key_grad, value_grad = query_grad.T, key_grad.T, value_grad.T
     terms = terms_all[:, 0, :]
     chosen = (gathered[:, 0, head_count].astype(jnp.int32)[:, None] == levels[None, :]).astype(f32)

time: 178 us -> 171 us (0.961)
  local copies, waits for them, and re-layouts: 19.9 us -> 15 us
  Pallas kernels: 145 us -> 141 us
  other arithmetic: 6.92 us -> 9.17 us
    pallas_call x3, Pallas kernels: 59.7 us -> 43.5 us  [local_call(): pl.pallas_call(kernel, out_shape=tuple(outs), in_specs=[pl.BlockSpec(memo...]
    pallas_call x2 -> x3, Pallas kernels: 71.5 us -> 83.6 us  [the longest x2 81.3 us: carried(): pl.pallas_call(functools.partial(scan_kernel, n, rows, heads, depth, reve...]
    dynamic_update_slice x1 -> x0, local copies, waits for them, and re-layouts: 6.97 us -> none  [body(): lax.dynamic_update_slice(value_grad, jnp.stack(fixed, axis=1).astype(bf16...]
    unnamed x23 -> x48, local copies, waits for them, and re-layouts: 4.05 us -> 6.57 us
  transfers between devices with their start and end apart: 1 -> 1, of which waited for: 0 -> 0; matrix products, arithmetic and copies ran while one was open for 2% -> 3% of each run, Pallas kernels for 0% -> 0%
where the time goes in v1:
time: 171 us
  Pallas kernels  141 us (82%)
  local copies, waits for them, and re-layouts  15 us (9%)
  other arithmetic  9.17 us (5%)
  starting transfers between devices  2.36 us (1%)
    pallas_call x2, Pallas kernels, carried(): pl.pallas_call(functools.partial(scan_kernel, n, rows, heads, depth, reve...  81.3 us
    pallas_call x3, Pallas kernels, local_call(): pl.pallas_call(kernel, out_shape=tuple(outs), in_specs=[pl.BlockSpec(memo...  43.5 us
    pallas_call x1, Pallas kernels, tail_exchange(): pl.pallas_call(functools.partial(tail_kernel, n), out_shape=(jax.ShapeDty...  14.1 us
    unnamed x48, local copies, waits for them, and re-layouts  6.57 us
  transfers between devices with their start and end apart: 1, of which 0 were waited for; matrix products, arithmetic and copies ran while one was open for 3% of the time, Pallas kernels for 0%

profile of v1, /device:TPU:0, one launch (start us, length us, event | category | flops | bytes accessed | tf_op | source)
XLA Modules:
  0.0 170.7 jit_solution(18178309667586513318)
XLA Ops:
  0.7 1.3 slice.45
  2.2 2.4 %collective-permute-start = (bf16[3,2240]{1,0:T(4,128)(2,1)S(1)}, bf16[3,2240]{1,0:T(4,128)(2,1)S(1)}, u32[]{:S(2)}, u32[]{:S(2)}) collective-permute-start(bf16[3,2240]{1,0:T(4,128)(2,1)S(1)} %copy.45), channel_id=1, source_target_pairs={{0,1},{1,2},{2,3},{3,4},{4,5},{5,6},{6,7},{7,8},{8,9},{9,10},{10,1... | collective-permute-start | bytes 40328 | tf_op jit(solution)/shard_map/ppermute | solution.py:182
  5.4 0.9 add_multiply_fusion
  6.3 1.2 and_select_fusion
  7.5 0.6 pad_maximum_fusion.2.scal.refs_2_.refs_3_
  8.2 1.4 copy.40
  9.9 1.0 pad.8.before
  11.0 0.6 iota.21.late.refs_4_
  11.6 10.0 %conv_state.1 = (bf16[2240,384]{1,0:T(8,128)(2,1)}, bf16[2304,112]{1,0:T(8,128)(2,1)}) custom-call(f32[3,20]{1,0:T(4,128)} %pad_maximum_fusion.2.scal.refs_2_.refs_3_, bf16[112,384]{1,0:T(8,128)(2,1)} %iota.21.late.refs_4_, bf16[2240,384]{1,0:T(8,128)(2,1)} %bitcast.70, bf16[2240,384]{1,0:T(8,128)(2,1)} %bitcast.86, bf16[2240,128]{1,0:T(8,128)(2,1)} %pad.8.before, ...), custom_call_target="tpu_custom_call" | custom-call | tf_op jit(solution)/shard_map/conv_state/pallas_call | solution.py:299
  21.6 1.1 copy-done.13
  22.7 32.2 %state_scan.1 = (bf16[16,144,112]{2,1,0:T(8,128)(2,1)S(1)}, f32[16,1,128]{2,1,0:T(1,128)S(1)}, f32[2240,384]{1,0:T(8,128)}) custom-call(bf16[16,144,112]{2,1,0:T(8,128)(2,1)S(1)} %bitcast.82, f32[1,128]{1,0:T(1,128)S(1)} %maximum_bitcast_fusion.refs_1_, f32[3,20]{1,0:T(4,128)S(1)} %copy-done.14, f32[384,384]{1,0:T(8,128)S(1)} %copy-done.4, ...), custom_call_target="tpu_custom_call" | custom-call | tf_op jit(solution)/shard_map/state_scan/pallas_call | solution.py:112
  54.9 0.8 copy-done.6
  55.7 0.4 convert_reduce_fusion
  56.2 12.4 %heads.1 = (bf16[2240,384]{1,0:T(8,128)(2,1)}, bf16[2304,112]{1,0:T(8,128)(2,1)}, f32[2240,1]{1,0:T(8,128)}) custom-call(f32[3,20]{1,0:T(4,128)} %pad_maximum_fusion.2.scal.refs_2_.refs_3_, bf16[112,384]{1,0:T(8,128)(2,1)} %iota.21.late.refs_4_, bf16[2240,384]{1,0:T(8,128)(2,1)} %bitcast.74, f32[2240,384]{1,0:T(8,128)} %get-tuple-element.28.part, ...), custom_call_target="tpu_custom_call" | custom-call | tf_op jit(solution)/shard_map/heads/pallas_call | solution.py:299
  68.6 1.6 reduce
  70.3 1.1 copy-done.12
  71.4 49.1 %adjoint_scan.1 = (bf16[16,144,112]{2,1,0:T(8,128)(2,1)S(1)}, f32[16,1,2240]{2,1,0:T(1,128)S(1)}, bf16[2240,384]{1,0:T(8,128)(2,1)S(1)}, f32[2240,384]{1,0:T(8,128)}, f32[2240,384]{1,0:T(8,128)}) custom-call(bf16[16,144,112]{2,1,0:T(8,128)(2,1)S(1)} %bitcast.81, f32[1,2240]{1,0:T(1,128)S(1)} %reshape.100.refs_1_, ...), custom_call_target="tpu_custom_call" | custom-call | tf_op jit(solution)/shard_map/adjoint_scan/pallas_call | solution.py:112
  120.5 1.3 copy-done.9
  121.8 0.8 copy-done.11
  122.6 21.1 %adjoint_terms.1 = (bf16[2240,384]{1,0:T(8,128)(2,1)}, bf16[2240,384]{1,0:T(8,128)(2,1)}, f32[2240,4]{1,0:T(8,128)}, f32[2240,128]{1,0:T(8,128)}, f32[2240,128]{1,0:T(8,128)}) custom-call(f32[3,20]{1,0:T(4,128)} %pad_maximum_fusion.2.scal.refs_2_.refs_3_, bf16[112,384]{1,0:T(8,128)(2,1)} %iota.21.late.refs_4_, bf16[2240,384]{1,0:T(8,128)(2,1)} %bitcast.72, ...), custom_call_target="tpu_custom_call" | custom-call | tf_op jit(solution)/shard_map/adjoint_terms/pallas_call | solution.py:299
  143.7 2.3 %copy.41 = f32[2240,4]{0,1:T(4,128)} copy(f32[2240,4]{1,0:T(8,128)} %get-tuple-element.41) | data formatting | bytes 71680 | tf_op jit(solution)/shard_map/adjoint_terms/pallas_call | solution.py:299
  146.1 1.4 multiply_multiply_fusion
  147.4 0.6 broadcast_multiply_fusion.1
  148.0 0.4 copy.42
  148.4 0.6 slice_bitcast_fusion.edge
  149.0 14.1 %tail_exchange.1 = (f32[4,2240]{1,0:T(4,128)}, f32[3,2240]{1,0:T(4,128)}) custom-call(f32[4,2240]{1,0:T(4,128)} %bitcast.91, f32[3,2240]{1,0:T(4,128)} %slice_bitcast_fusion.edge), custom_call_target="tpu_custom_call" | custom-call | tf_op jit(solution)/shard_map/tail_exchange/pallas_call | solution.py:162
  163.2 0.8 select_bitcast_fusion
  164.0 1.4 broadcast_multiply_fusion
  165.5 0.4 copy.43
  165.9 1.4 pad_add_fusion.tile
  167.2 2.3 %last_tokens.1 = bf16[2240,384]{1,0:T(8,128)(2,1)} custom-call(bf16[2240,384]{1,0:T(8,128)(2,1)} %get-tuple-element.39.whole, f32[2240,128]{1,0:T(8,128)} %pad_add_fusion.tile), custom_call_target="tpu_custom_call", output_to_operand_aliasing={{}: (0, {})} | custom-call | tf_op jit(solution)/shard_map/last_tokens/pallas_call | solution.py:385
  169.5 1.2 copy.55
  (54 shorter events, 1.0 us)
Async XLA Ops:
  0.6 4.0 %copy-start.22 = (s32[1,2]{1,0:T(1,128)S(1)}, s32[1,2]{1,0:T(1,128)}, u32[]{:S(2)}) copy-start(s32[1,2]{1,0:T(1,128)} %param.13) | copy-start | bytes 28
  0.6 4.1 %copy-start.21 = (f32[1,2,20]{2,1,0:T(2,128)S(1)}, f32[1,2,20]{2,1,0:T(2,128)}, u32[]{:S(2)}) copy-start(f32[1,2,20]{2,1,0:T(2,128)} %param.14) | copy-start | bytes 484
  0.7 4.7 %copy-start.20 = (f32[2240]{0:T(1024)S(1)}, f32[2240]{0:T(1024)}, u32[]{:S(2)}) copy-start(f32[2240]{0:T(1024)} %param.17) | copy-start | bytes 26884
  0.7 5.6 %copy-start.19 = (f32[4,2240]{1,0:T(4,128)S(1)}, f32[4,2240]{1,0:T(4,128)}, u32[]{:S(2)}) copy-start(f32[4,2240]{1,0:T(4,128)} %param.16) | copy-start | bytes 107524
  2.2 7.4 %collective-permute-start = (bf16[3,2240]{1,0:T(4,128)(2,1)S(1)}, bf16[3,2240]{1,0:T(4,128)(2,1)S(1)}, u32[]{:S(2)}, u32[]{:S(2)}) collective-permute-start(bf16[3,2240]{1,0:T(4,128)(2,1)S(1)} %copy.45), channel_id=1, source_target_pairs={{0,1},{1,2},{2,3},{3,4},{4,5},{5,6},{6,7},{7,8},{8,9},{9,10},{10,1... | collective-permute-start | bytes 40328 | tf_op jit(solution)/shard_map/ppermute | solution.py:182
  11.6 10.0 %copy-start = (bf16[384,2240]{0,1:T(8,128)(2,1)S(1)}, bf16[384,2240]{0,1:T(8,128)(2,1)}, u32[]{:S(2)}) copy-start(bf16[384,2240]{0,1:T(8,128)(2,1)} %param.11) | copy-start | bytes 5160964
  11.6 10.0 %copy-start.1 = (bf16[384,2240]{0,1:T(8,128)(2,1)S(1)}, bf16[384,2240]{0,1:T(8,128)(2,1)}, u32[]{:S(2)}) copy-start(bf16[384,2240]{0,1:T(8,128)(2,1)} %param.10) | copy-start | bytes 5160964
  11.6 10.0 %copy-start.2 = (f32[384,384]{1,0:T(8,128)S(1)}, f32[384,384]{1,0:T(8,128)}, u32[]{:S(2)}) copy-start(f32[384,384]{1,0:T(8,128)} %get-tuple-element.54.refs_4_.refs_6_) | copy-start | bytes 1769476
  11.6 10.0 %copy-start.4 = (f32[384,384]{1,0:T(8,128)S(1)}, f32[384,384]{1,0:T(8,128)}, u32[]{:S(2)}) copy-start(f32[384,384]{1,0:T(8,128)} %get-tuple-element.55.refs_3_.refs_5_) | copy-start | bytes 1769476
  11.6 10.0 %copy-start.14 = (f32[3,20]{1,0:T(4,128)S(1)}, f32[3,20]{1,0:T(4,128)}, u32[]{:S(2)}) copy-start(f32[3,20]{1,0:T(4,128)} %pad_maximum_fusion.2.scal.refs_2_.refs_3_) | copy-start | bytes 724
  21.6 1.1 copy-start.13
  54.9 0.9 copy-start.6
  56.2 14.1 %copy-start.3 = (f32[384,384]{1,0:T(8,128)S(1)}, f32[384,384]{1,0:T(8,128)}, u32[]{:S(2)}) copy-start(f32[384,384]{1,0:T(8,128)} %get-tuple-element.54.refs_4_.refs_6_) | copy-start | bytes 1769476
  56.2 14.1 %copy-start.5 = (f32[384,384]{1,0:T(8,128)S(1)}, f32[384,384]{1,0:T(8,128)}, u32[]{:S(2)}) copy-start(f32[384,384]{1,0:T(8,128)} %get-tuple-element.55.refs_3_.refs_5_) | copy-start | bytes 1769476
  56.2 14.1 %copy-start.7 = (bf16[16,144,112]{2,1,0:T(8,128)(2,1)S(1)}, bf16[16,144,112]{2,1,0:T(8,128)(2,1)}, u32[]{:S(2)}) copy-start(bf16[16,144,112]{2,1,0:T(8,128)(2,1)} %copy-done.6) | copy-start | bytes 1548292
  56.2 14.1 %copy-start.8 = (bf16[112,384]{1,0:T(8,128)(2,1)S(1)}, bf16[112,384]{1,0:T(8,128)(2,1)}, u32[]{:S(2)}) copy-start(bf16[112,384]{1,0:T(8,128)(2,1)} %iota.21.late.refs_4_) | copy-start | bytes 258052
  56.2 14.1 %copy-start.15 = (f32[3,20]{1,0:T(4,128)S(1)}, f32[3,20]{1,0:T(4,128)}, u32[]{:S(2)}) copy-start(f32[3,20]{1,0:T(4,128)} %pad_maximum_fusion.2.scal.refs_2_.refs_3_) | copy-start | bytes 724
  70.3 1.1 copy-start.12
  120.5 1.3 copy-start.9
  121.8 0.8 copy-start.11
  122.6 23.5 %copy-start.18 = (f32[50,2240]{1,0:T(8,128)S(1)}, f32[50,2240]{1,0:T(8,128)}, u32[]{:S(2)}) copy-start(f32[50,2240]{1,0:T(8,128)} %param.18) | copy-start | bytes 1344004
  143.7 4.3 %copy-start.16 = (f32[2240,128]{1,0:T(8,128)S(1)}, f32[2240,128]{1,0:T(8,128)}, u32[]{:S(2)}) copy-start(f32[2240,128]{1,0:T(8,128)} %get-tuple-element.42) | copy-start | bytes 3440644
  148.4 17.4 %copy-start.17 = (f32[2240,128]{1,0:T(8,128)S(1)}, f32[2240,128]{1,0:T(8,128)}, u32[]{:S(2)}) copy-start(f32[2240,128]{1,0:T(8,128)} %get-tuple-element.40) | copy-start | bytes 3440644
  167.2 2.3 %copy-start.10 = (bf16[2240,384]{1,0:T(8,128)(2,1)S(1)}, bf16[2240,384]{1,0:T(8,128)(2,1)}, u32[]{:S(2)}) copy-start(bf16[2240,384]{1,0:T(8,128)(2,1)} %copy-done.9) | copy-start | bytes 5160964

commit v2 on v1

--- a/solution.py
+++ b/solution.py
@@ -204,6 +204,16 @@
         work(stop - 1, pl.ds((stop - 1) * dim, dim))
 
 
+def heads_per_step(heads):
+    return next(k for k in (4, 2, 1) if heads % k == 0)
+
+
+def step_heads(heads, dim, work):
+    count = heads_per_step(heads)
+    for j in range(count):
+        work(pl.program_id(0) * count + j, slice(j * dim, (j + 1) * dim))
+
+
 def delayed(value, before, taps):
     count = value.shape[1]
     joined = jnp.concatenate([before, value], axis=1)
@@ -222,8 +232,7 @@
         conv[c, :] = v
         state[c, :] = framed_outer(v, key[c, :], late[...], scal[0, h], 1.0)
 
-    per_head(0, heads, dim, work)
-    state[heads * dim :, :] = jnp.zeros_like(state[heads * dim :, :])
+    step_heads(heads, dim, work)
 
 
 def ahead_work(scal, same, cross, query, key, conv, part, h, c):
@@ -261,8 +270,7 @@
         grad[c, :] = g
         adjoint[c, :] = framed_outer(g, q, late[...], scal[1, h], scal[2, h])
 
-    per_head(0, heads, dim, work)
-    adjoint[heads * dim :, :] = jnp.zeros_like(adjoint[heads * dim :, :])
+    step_heads(heads, dim, work)
 
 
 def post_kernel(heads, dim, tap_count, scal, late, key, conv, value, before, columns, adjoint, key_part,
@@ -287,22 +295,28 @@
         grad_value[c, :] = total.astype(jnp.bfloat16)
         ending[c, :] = total[:, count - 128 :]
 
-    per_head(0, heads, dim, work)
+    step_heads(heads, dim, work)
 
 
 def end_kernel(whole, tile, out):
     out[...] = tile[...].astype(jnp.bfloat16)
 
 
-def local_call(kernel, name, args, outs, scratch=()):
-    vmem = pl.BlockSpec(memory_space=pltpu.VMEM)
+def local_call(kernel, name, heads, dim, args, outs):
+    rows = heads_per_step(heads) * dim
+
+    def spec(array):
+        if array.shape[0] >= heads * dim:
+            return pl.BlockSpec((rows, array.shape[1]), lambda i: (i, 0))
+        return pl.BlockSpec(array.shape, lambda i: (0, 0))
+
     return pl.pallas_call(
         kernel,
+        grid=(heads * dim // rows,),
         out_shape=tuple(outs),
-        in_specs=[pl.BlockSpec(memory_space=pltpu.SMEM)] + [vmem] * (len(args) - 1),
-        out_specs=tuple([vmem] * len(outs)),
-        scratch_shapes=list(scratch),
-        compiler_params=pltpu.CompilerParams(vmem_limit_bytes=56 << 20),
+        in_specs=[pl.BlockSpec(memory_space=pltpu.SMEM)] + [spec(a) for a in args[1:]],
+        out_specs=tuple(spec(a) for a in outs),
+        compiler_params=pltpu.CompilerParams(vmem_limit_bytes=40 << 20),
         name=name,
     )(*args)
 
@@ -354,14 +368,14 @@
     sizes = (head_count, head_dim, tap_count)
     whole = (channels, row_count)
     conv_values, local_state = local_call(
-        functools.partial(pre_kernel, *sizes), "conv_state",
+        functools.partial(pre_kernel, *sizes), "conv_state", head_count, head_dim,
         (scal, late, key_t, value_t, before, columns),
         (shape(whole, bf16), shape((state_rows, head_dim), bf16)))
     state_in, gathered, part = carried(
         local_state, lanes, None, head_count, head_dim, False, ahead_work,
         (scal, same, cross, query_t, key_t, conv_values), (shape(whole, f32),))
     grad, adjoint_local, block_terms = local_call(
-        functools.partial(mid_kernel, *sizes), "heads",
+        functools.partial(mid_kernel, *sizes), "heads", head_count, head_dim,
         (scal, late, query_t, part, upstream_t, columns, state_in),
         (shape(whole, bf16), shape((state_rows, head_dim), bf16), shape((channels, 1), f32)))
     adjoint, terms_all, query_grad, key_part, value_part = carried(
@@ -369,7 +383,7 @@
         (scal, late, same, cross, query_t, key_t, conv_values, grad, state_in),
         (shape(whole, bf16), shape(whole, f32), shape(whole, f32)))
     key_grad, value_grad, tap_terms, opening, ending = local_call(
-        functools.partial(post_kernel, *sizes), "adjoint_terms",
+        functools.partial(post_kernel, *sizes), "adjoint_terms", head_count, head_dim,
         (scal, late, key_t, conv_values, value_t, before, columns, adjoint, key_part, value_part),
         (shape(whole, bf16), shape(whole, bf16), shape((channels, tap_count), f32),
          shape((channels, 128), f32), shape((channels, 128), f32)))

time: 171 us -> 164 us (0.959)
  Pallas kernels: 141 us -> 125 us
  local copies, waits for them, and re-layouts: 15 us -> 22.5 us
    pallas_call x3, Pallas kernels: 43.5 us -> 27.7 us  [local_call(): pl.pallas_call(kernel, grid=(heads * dim // rows,), out_shape=tuple(outs)...]
    unnamed x48 -> x64, local copies, waits for them, and re-layouts: 6.57 us -> 15.3 us
  transfers between devices with their start and end apart: 1 -> 1, of which waited for: 0 -> 0; matrix products, arithmetic and copies ran while one was open for 3% -> 2% of each run, Pallas kernels for 0% -> 0%
where the time goes in v2:
time: 164 us
  Pallas kernels  125 us (76%)
  local copies, waits for them, and re-layouts  22.5 us (14%)
  other arithmetic  8.92 us (5%)
  starting transfers between devices  2.96 us (2%)
  matrix products  2.41 us (1%)
  between operations  1.65 us (1%)
    pallas_call x2, Pallas kernels, carried(): pl.pallas_call(functools.partial(scan_kernel, n, rows, heads, depth, reve...  81 us
    pallas_call x3, Pallas kernels, local_call(): pl.pallas_call(kernel, grid=(heads * dim // rows,), out_shape=tuple(outs)...  27.7 us
    unnamed x64, local copies, waits for them, and re-layouts  15.3 us
    pallas_call x1, Pallas kernels, tail_exchange(): pl.pallas_call(functools.partial(tail_kernel, n), out_shape=(jax.ShapeDty...  14.1 us
  transfers between devices with their start and end apart: 1, of which 0 were waited for; matrix products, arithmetic and copies ran while one was open for 2% of the time, Pallas kernels for 0%

profile of v2, /device:TPU:0, one launch (start us, length us, event | category | flops | bytes accessed | tf_op | source)
XLA Modules:
  0.0 163.6 jit_solution(16470401649336669920)
XLA Ops:
  0.7 1.3 slice.45
  2.0 0.9 copy.45
  2.8 3.0 %collective-permute-start = (bf16[3,2240]{1,0:T(4,128)(2,1)}, bf16[3,2240]{1,0:T(4,128)(2,1)}, u32[]{:S(2)}, u32[]{:S(2)}) collective-permute-start(bf16[3,2240]{1,0:T(4,128)(2,1)} %copy.45), channel_id=1, source_target_pairs={{0,1},{1,2},{2,3},{3,4},{4,5},{5,6},{6,7},{7,8},{8,9},{9,10},{10,1... | collective-permute-start | bytes 40328 | tf_op jit(solution)/shard_map/ppermute | solution.py:182
  6.6 0.9 add_multiply_fusion
  7.5 1.0 and_select_fusion
  9.6 1.8 %copy.39 = bf16[3,2240]{0,1:T(8,128)(2,1)} copy(bf16[3,2240]{1,0:T(4,128)(2,1)} %collective-permute-done) | data formatting | bytes 26880 | tf_op jit(solution)/shard_map/ppermute | solution.py:182
  11.4 1.3 pad.8.before
  12.7 1.6 %copy-done.5 = bf16[384,2240]{0,1:T(8,128)(2,1)S(1)} copy-done((bf16[384,2240]{0,1:T(8,128)(2,1)S(1)}, bf16[384,2240]{0,1:T(8,128)(2,1)}, u32[]{:S(2)}) %copy-start.5) | copy-done | bytes 1720344
  14.4 6.0 %conv_state.1 = (bf16[2240,384]{1,0:T(8,128)(2,1)S(1)}, bf16[2304,112]{1,0:T(8,128)(2,1)S(1)}) custom-call(f32[3,20]{1,0:T(4,128)S(1)} %pad_maximum_fusion.2.scal.refs_2_.refs_3_, bf16[112,384]{1,0:T(8,128)(2,1)S(1)} %iota.21.late.refs_4_, bf16[2240,384]{1,0:T(8,128)(2,1)S(1)} %bitcast.71, bf16[2240,384]{1,0:T(8,128)(2,1)S(1)} %bitcast.80, ...), custom_call_target="tpu_custom_call" | custom-call | tf_op jit(solution)/shard_map/conv_state/pallas_call | solution.py:313
  20.4 1.2 copy-done.2
  21.6 31.7 %state_scan.1 = (bf16[16,144,112]{2,1,0:T(8,128)(2,1)S(1)}, f32[16,1,128]{2,1,0:T(1,128)S(1)}, f32[2240,384]{1,0:T(8,128)}) custom-call(bf16[16,144,112]{2,1,0:T(8,128)(2,1)S(1)} %bitcast.88, f32[1,128]{1,0:T(1,128)S(1)} %copy-done.24, f32[3,20]{1,0:T(4,128)S(1)} %pad_maximum_fusion.2.scal.refs_2_.refs_3_, f32[384,384]{1,0:T(8,128)S(1)} %copy-done.7, ...), custom_call_target="tpu_custom_call" | custom-call | tf_op jit(solution)/shard_map/state_scan/pallas_call | solution.py:112
  53.8 2.0 %copy-done.12 = f32[2240,384]{1,0:T(8,128)S(1)} copy-done((f32[2240,384]{1,0:T(8,128)S(1)}, f32[2240,384]{1,0:T(8,128)}, u32[]{:S(2)}) %copy-start.12) | copy-done | bytes 3440664
  55.8 7.4 %heads.1 = (bf16[2240,384]{1,0:T(8,128)(2,1)S(1)}, bf16[2304,112]{1,0:T(8,128)(2,1)S(1)}, f32[2240,1]{1,0:T(8,128)S(1)}) custom-call(f32[3,20]{1,0:T(4,128)S(1)} %pad_maximum_fusion.2.scal.refs_2_.refs_3_, bf16[112,384]{1,0:T(8,128)(2,1)S(1)} %iota.21.late.refs_4_, bf16[2240,384]{1,0:T(8,128)(2,1)S(1)} %bitcast.79, f32[2240,384]{1,0:T(8,128)S(1)} %copy-done.12, ...), custom_call_target="tpu_custom_call" | custom-call | tf_op jit(solution)/shard_map/heads/pallas_call | solution.py:313
  63.2 1.2 copy-done.15
  64.4 1.0 copy-done.21
  65.4 1.6 reduce
  67.1 1.1 copy-done.14
  68.1 49.3 %adjoint_scan.1 = (bf16[16,144,112]{2,1,0:T(8,128)(2,1)S(1)}, f32[16,1,2240]{2,1,0:T(1,128)S(1)}, bf16[2240,384]{1,0:T(8,128)(2,1)S(1)}, f32[2240,384]{1,0:T(8,128)}, f32[2240,384]{1,0:T(8,128)}) custom-call(bf16[16,144,112]{2,1,0:T(8,128)(2,1)S(1)} %bitcast.87, f32[1,2240]{1,0:T(1,128)S(1)} %reshape.100.refs_1_, ...), custom_call_target="tpu_custom_call" | custom-call | tf_op jit(solution)/shard_map/adjoint_scan/pallas_call | solution.py:112
  117.4 1.2 copy-done.17
  118.6 2.0 %copy-done.11 = f32[2240,384]{1,0:T(8,128)S(1)} copy-done((f32[2240,384]{1,0:T(8,128)S(1)}, f32[2240,384]{1,0:T(8,128)}, u32[]{:S(2)}) %copy-start.11) | copy-done | bytes 3440664
  120.6 14.3 %adjoint_terms.1 = (bf16[2240,384]{1,0:T(8,128)(2,1)}, bf16[2240,384]{1,0:T(8,128)(2,1)}, f32[2240,4]{1,0:T(8,128)S(1)}, f32[2240,128]{1,0:T(8,128)S(1)}, f32[2240,128]{1,0:T(8,128)S(1)}) custom-call(f32[3,20]{1,0:T(4,128)S(1)} %pad_maximum_fusion.2.scal.refs_2_.refs_3_, bf16[112,384]{1,0:T(8,128)(2,1)S(1)} %iota.21.late.refs_4_, ...), custom_call_target="tpu_custom_call" | custom-call | tf_op jit(solution)/shard_map/adjoint_terms/pallas_call | solution.py:313
  134.9 1.0 copy-done.19
  135.9 1.0 copy-done.22
  136.9 1.0 copy.41
  137.9 2.4 %multiply_multiply_fusion = (f32[50,2240]{1,0:T(8,128)}, f32[2240]{0:T(1024)S(1)}) fusion(f32[2240]{0:T(1024)S(1)} %copy-done.28, f32[50,2240]{1,0:T(8,128)} %param.18, f32[16,1,2240]{2,1,0:T(1,128)S(1)} %get-tuple-element.45, s32[16]{0:T(128)S(1)} %convert_reduce_fusion), kind=kOutput, calls=%fused_computation.3 | convolution fusion | flops 22062560 | bytes 1057344 | tf_op jit(solution)/shard_map/bl,bc->lc/dot_general | solution.py:411
  141.3 0.6 slice_bitcast_fusion.edge
  141.9 14.1 %tail_exchange.1 = (f32[4,2240]{1,0:T(4,128)}, f32[3,2240]{1,0:T(4,128)}) custom-call(f32[4,2240]{1,0:T(4,128)} %bitcast.91, f32[3,2240]{1,0:T(4,128)} %slice_bitcast_fusion.edge), custom_call_target="tpu_custom_call" | custom-call | tf_op jit(solution)/shard_map/tail_exchange/pallas_call | solution.py:162
  156.0 0.8 select_bitcast_fusion
  156.9 1.4 broadcast_multiply_fusion
  158.7 1.4 pad_add_fusion.tile
  160.1 2.3 %last_tokens.1 = bf16[2240,384]{1,0:T(8,128)(2,1)} custom-call(bf16[2240,384]{1,0:T(8,128)(2,1)} %get-tuple-element.39.whole, f32[2240,128]{1,0:T(8,128)} %pad_add_fusion.tile), custom_call_target="tpu_custom_call", output_to_operand_aliasing={{}: (0, {})} | custom-call | tf_op jit(solution)/shard_map/last_tokens/pallas_call | solution.py:399
  162.4 1.2 copy.55
  (70 shorter events, 3.1 us)
Async XLA Ops:
  0.6 5.2 %copy-start.30 = (s32[1,2]{1,0:T(1,128)S(1)}, s32[1,2]{1,0:T(1,128)}, u32[]{:S(2)}) copy-start(s32[1,2]{1,0:T(1,128)} %param.13) | copy-start | bytes 28
  0.6 5.3 %copy-start.29 = (f32[1,2,20]{2,1,0:T(2,128)S(1)}, f32[1,2,20]{2,1,0:T(2,128)}, u32[]{:S(2)}) copy-start(f32[1,2,20]{2,1,0:T(2,128)} %param.14) | copy-start | bytes 484
  0.7 5.9 %copy-start.27 = (f32[2240]{0:T(1024)S(1)}, f32[2240]{0:T(1024)}, u32[]{:S(2)}) copy-start(f32[2240]{0:T(1024)} %param.17) | copy-start | bytes 26884
  0.7 6.8 %copy-start.25 = (f32[4,2240]{1,0:T(4,128)S(1)}, f32[4,2240]{1,0:T(4,128)}, u32[]{:S(2)}) copy-start(f32[4,2240]{1,0:T(4,128)} %param.16) | copy-start | bytes 107524
  2.8 6.7 %collective-permute-start = (bf16[3,2240]{1,0:T(4,128)(2,1)}, bf16[3,2240]{1,0:T(4,128)(2,1)}, u32[]{:S(2)}, u32[]{:S(2)}) collective-permute-start(bf16[3,2240]{1,0:T(4,128)(2,1)} %copy.45), channel_id=1, source_target_pairs={{0,1},{1,2},{2,3},{3,4},{4,5},{5,6},{6,7},{7,8},{8,9},{9,10},{10,1... | collective-permute-start | bytes 40328 | tf_op jit(solution)/shard_map/ppermute | solution.py:182
  8.5 4.2 %copy-start = (bf16[384,2240]{0,1:T(8,128)(2,1)S(1)}, bf16[384,2240]{0,1:T(8,128)(2,1)}, u32[]{:S(2)}) copy-start(bf16[384,2240]{0,1:T(8,128)(2,1)} %param.11) | copy-start | bytes 5160964
  12.7 7.7 %copy-start.9 = (bf16[2240,128]{1,0:T(8,128)(2,1)}, bf16[2240,128]{1,0:T(8,128)(2,1)S(1)}, u32[]{:S(2)}) copy-start(bf16[2240,128]{1,0:T(8,128)(2,1)S(1)} %pad.8.before) | copy-start | bytes 1720324
  12.7 1.7 %copy-start.5 = (bf16[384,2240]{0,1:T(8,128)(2,1)S(1)}, bf16[384,2240]{0,1:T(8,128)(2,1)}, u32[]{:S(2)}) copy-start(bf16[384,2240]{0,1:T(8,128)(2,1)} %param.12) | copy-start | bytes 5160964
  14.3 7.3 %copy-start.4 = (bf16[384,2240]{0,1:T(8,128)(2,1)S(1)}, bf16[384,2240]{0,1:T(8,128)(2,1)}, u32[]{:S(2)}) copy-start(bf16[384,2240]{0,1:T(8,128)(2,1)} %param.10) | copy-start | bytes 5160964
  14.4 7.3 %copy-start.7 = (f32[384,384]{1,0:T(8,128)S(1)}, f32[384,384]{1,0:T(8,128)}, u32[]{:S(2)}) copy-start(f32[384,384]{1,0:T(8,128)} %get-tuple-element.55.refs_3_.refs_5_) | copy-start | bytes 1769476
  14.4 7.3 %copy-start.24 = (f32[1,128]{1,0:T(1,128)S(1)}, f32[1,128]{1,0:T(1,128)}, u32[]{:S(2)}) copy-start(f32[1,128]{1,0:T(1,128)} %maximum_bitcast_fusion.refs_1_) | copy-start | bytes 1540
  20.4 1.2 copy-start.2
  21.6 32.2 %copy-start.16 = (bf16[384,2240]{0,1:T(8,128)(2,1)S(1)}, bf16[384,2240]{0,1:T(8,128)(2,1)}, u32[]{:S(2)}) copy-start(bf16[384,2240]{0,1:T(8,128)(2,1)} %param.19) | copy-start | bytes 5160964
  53.3 9.8 %copy-start.13 = (bf16[16,144,112]{2,1,0:T(8,128)(2,1)}, bf16[16,144,112]{2,1,0:T(8,128)(2,1)S(1)}, u32[]{:S(2)}) copy-start(bf16[16,144,112]{2,1,0:T(8,128)(2,1)S(1)} %get-tuple-element.29) | copy-start | bytes 1548292
  53.8 2.0 %copy-start.12 = (f32[2240,384]{1,0:T(8,128)S(1)}, f32[2240,384]{1,0:T(8,128)}, u32[]{:S(2)}) copy-start(f32[2240,384]{1,0:T(8,128)} %get-tuple-element.28.part) | copy-start | bytes 10321924
  55.8 11.2 %copy-start.8 = (f32[384,384]{1,0:T(8,128)S(1)}, f32[384,384]{1,0:T(8,128)}, u32[]{:S(2)}) copy-start(f32[384,384]{1,0:T(8,128)} %get-tuple-element.55.refs_3_.refs_5_) | copy-start | bytes 1769476
  63.2 1.2 copy-start.15
  64.4 1.0 copy-start.21
  67.0 1.1 copy-start.14
  68.1 50.5 %copy-start.1 = (bf16[384,2240]{0,1:T(8,128)(2,1)S(1)}, bf16[384,2240]{0,1:T(8,128)(2,1)}, u32[]{:S(2)}) copy-start(bf16[384,2240]{0,1:T(8,128)(2,1)} %param.11) | copy-start | bytes 5160964
  68.1 50.5 %copy-start.3 = (bf16[2240,384]{1,0:T(8,128)(2,1)S(1)}, bf16[2240,384]{1,0:T(8,128)(2,1)}, u32[]{:S(2)}) copy-start(bf16[2240,384]{1,0:T(8,128)(2,1)} %copy-done.2) | copy-start | bytes 5160964
  68.1 50.5 %copy-start.6 = (bf16[384,2240]{0,1:T(8,128)(2,1)S(1)}, bf16[384,2240]{0,1:T(8,128)(2,1)}, u32[]{:S(2)}) copy-start(bf16[384,2240]{0,1:T(8,128)(2,1)} %param.12) | copy-start | bytes 5160964
  68.1 50.5 %copy-start.10 = (bf16[2240,128]{1,0:T(8,128)(2,1)S(1)}, bf16[2240,128]{1,0:T(8,128)(2,1)}, u32[]{:S(2)}) copy-start(bf16[2240,128]{1,0:T(8,128)(2,1)} %copy-done.9) | copy-start | bytes 1720324
  117.4 1.2 copy-start.17
  118.6 2.0 %copy-start.11 = (f32[2240,384]{1,0:T(8,128)S(1)}, f32[2240,384]{1,0:T(8,128)}, u32[]{:S(2)}) copy-start(f32[2240,384]{1,0:T(8,128)} %get-tuple-element.36.key_part) | copy-start | bytes 10321924
  120.6 17.3 %copy-start.28 = (f32[2240]{0:T(1024)S(1)}, f32[2240]{0:T(1024)}, u32[]{:S(2)}) copy-start(f32[2240]{0:T(1024)} %param.17) | copy-start | bytes 26884
  134.9 1.0 copy-start.19
  135.9 1.0 copy-start.22
  136.9 4.0 %copy-start.20 = (f32[2240,128]{1,0:T(8,128)S(1)}, f32[2240,128]{1,0:T(8,128)}, u32[]{:S(2)}) copy-start(f32[2240,128]{1,0:T(8,128)} %copy-done.19) | copy-start | bytes 3440644
  137.9 18.9 %copy-start.26 = (f32[4,2240]{1,0:T(4,128)S(1)}, f32[4,2240]{1,0:T(4,128)}, u32[]{:S(2)}) copy-start(f32[4,2240]{1,0:T(4,128)} %param.16) | copy-start | bytes 107524
  140.9 17.8 %copy-start.23 = (f32[2240,128]{1,0:T(8,128)S(1)}, f32[2240,128]{1,0:T(8,128)}, u32[]{:S(2)}) copy-start(f32[2240,128]{1,0:T(8,128)} %copy-done.22) | copy-start | bytes 3440644
  160.1 2.3 %copy-start.18 = (bf16[2240,384]{1,0:T(8,128)(2,1)S(1)}, bf16[2240,384]{1,0:T(8,128)(2,1)}, u32[]{:S(2)}) copy-start(bf16[2240,384]{1,0:T(8,128)(2,1)} %copy-done.17) | copy-start | bytes 5160964
